TPU v7x, 32 devices: a whole 2x2x4 slice. The times are simulated.
32 devices in a mesh: sub: 4 (over z), wide: 8 (over y, x, core).
Axes of the slice: x: 2, y: 2, z: 4, core: 2. Of those that a mesh axis runs over, the one named last changes fastest.
Arguments:
- load_table: bfloat16 [4, 8, 16, 4, 128], P('sub', 'wide'), may hold values from -6 to 6
- load_column: int32 [64], replicated, may hold values from 0 to 15
- face_order: int32 [4, 8, 4], P('sub', 'wide'), may hold values from 0 to 3, each once within a row
- schur: bfloat16 [4, 8, 512, 512], P('sub', 'wide'), as said below
- neumann: bfloat16 [4, 8, 512, 512], P('sub', 'wide'), as said below
- coarse_basis: bfloat16 [4, 8, 4, 4, 128], P('sub', 'wide'), may hold values from -0.625 to 0.625
- corner_map: int32 [4, 8, 4], P('sub', 'wide'), may hold values from 0 to 47, as said below
- coarse_inverse: float32 [48, 48], P('wide'), as said below
Outputs:
- solution: float32 [4, 8, 4, 64, 128], P('sub', 'wide')
Inputs may be any that keep to these rules, and one draw needn't show every extreme that they name: `corner_map`: each subdomain's 4 entries are distinct; subdomains that meet at a corner of the grid of subdomains give it the same number, and different corners get different numbers, so (5) * (9) of the 48 numbers occur and the others belong to no corner. `coarse_inverse`: Symmetric. `schur`: Symmetric. `neumann`: Symmetric.
All inputs are finite; a program needn't handle non-finite values.
Results may differ from a plain program's by a relative error of at most 0.0014.
Values sent between devices are 32-bit elements; how exact they have to be, the bound alone decides.
A program may use at most 64 MiB of HBM per device.

v0:
```python
import jax
import jax.numpy as jnp
from jax import lax
from jax.sharding import PartitionSpec as P

ITERS = 3
damping = 0.3


def with_halo(cells, sides, width):
    for axis, dim in sides:
        count = lax.axis_size(axis)
        ends = count - 1
        head = lax.slice_in_dim(cells, 0, width, axis=dim)
        tail = lax.slice_in_dim(cells, cells.shape[dim] - width, cells.shape[dim], axis=dim)
        cells = jnp.concatenate(
            [
                lax.ppermute(tail, axis, [(i, (i + 1) % count) for i in range(ends)]),
                cells,
                lax.ppermute(head, axis, [((i + 1) % count, i) for i in range(ends)]),
            ],
            axis=dim,
        )
    return cells


def apply_local(vectors, operators, selector_half, selector_full):
    amount = vectors.shape[0]
    rhs_count = vectors.shape[3]
    face_width = vectors.shape[4]
    rounded = vectors.astype(jnp.bfloat16)
    blocked = jnp.einsum(
        "kcbf,kcfjn->kcjbn", selector_half, rounded, preferred_element_type=jnp.float32
    )
    blocked = blocked.astype(jnp.bfloat16).reshape(amount, 1, rhs_count, 4 * face_width)
    product = jnp.einsum("kcjm,kcmn->kcjn", blocked, operators, preferred_element_type=jnp.float32)
    product = product.reshape(amount, 1, rhs_count, 4, face_width)
    return jnp.einsum("kcbf,kcjbn->kcfjn", selector_full, product, precision=lax.Precision.HIGHEST)


def assemble(copies):
    side_stack = jnp.stack([copies[:, 0, 2], copies[:, 0, 3]], axis=0)
    side_halo = with_halo(side_stack, (("wide", 0),), 1)
    end_stack = jnp.stack([copies[0, 0, 0], copies[-1, 0, 1]], axis=0)
    end_halo = with_halo(end_stack, (("sub", 0),), 1)
    upper_faces = jnp.concatenate([end_halo[0:1], copies[:-1, 0, 1]], axis=0)
    lower_faces = jnp.concatenate([copies[1:, 0, 0], end_halo[3:4]], axis=0)
    north_sum = copies[:, 0, 0] + upper_faces
    south_sum = copies[:, 0, 1] + lower_faces
    west_sum = copies[:, 0, 2] + side_halo[0]
    east_sum = copies[:, 0, 3] + side_halo[3]
    return jnp.stack([north_sum, south_sum, west_sum, east_sum], axis=1)[:, None]


def coarse_solve(partial_value, coarse_inverse):
    assembled = lax.psum(partial_value, ("sub", "wide"))
    owned_rows = jnp.dot(assembled, coarse_inverse.T, precision=lax.Precision.HIGHEST)
    return lax.all_gather(owned_rows, "wide", axis=1, tiled=True)


def body(
    load_table, load_column, face_order, schur, neumann, coarse_basis, corner_map, coarse_inverse
):
    amount = schur.shape[0]
    pattern_count = load_table.shape[2]
    coarse_order = coarse_inverse.shape[1]
    selector_full = (face_order[..., :, None] == jnp.arange(4, dtype=jnp.int32)).astype(jnp.float32)
    selector_half = selector_full.astype(jnp.bfloat16)
    load_select = (load_column[:, None] == jnp.arange(pattern_count, dtype=jnp.int32)).astype(
        jnp.bfloat16
    )
    load_faces = jnp.einsum(
        "jl,kclfn->kcfjn", load_select, load_table, preferred_element_type=jnp.float32
    )
    row_ids = lax.axis_index("sub") * amount + jnp.arange(amount, dtype=jnp.int32)
    rows_total = amount * lax.axis_size("sub")
    column_index = lax.axis_index("wide") * jnp.ones((amount,), jnp.int32)
    cols_total = lax.axis_size("wide")
    half = jnp.float32(0.5)
    whole = jnp.float32(1.0)
    weights = jnp.stack(
        [
            jnp.where(row_ids > 0, half, whole),
            jnp.where(row_ids < rows_total - 1, half, whole),
            jnp.where(column_index > 0, half, whole),
            jnp.where(column_index < cols_total - 1, half, whole),
        ],
        axis=1,
    )[:, None, :, None, None]
    basis = coarse_basis.astype(jnp.float32)
    corner_marks = (corner_map[..., None] == jnp.arange(coarse_order, dtype=jnp.int32)).astype(
        jnp.float32
    )
    solution = jnp.zeros(load_faces.shape, jnp.float32)
    for iteration in range(ITERS):
        if iteration == 0:
            residual = assemble(load_faces)
        else:
            residual = assemble(
                load_faces - apply_local(solution, schur, selector_half, selector_full)
            )
        weighted = weights * residual
        restricted = jnp.einsum(
            "kcpfn,kcfjn->kcpj", basis, weighted, precision=lax.Precision.HIGHEST
        )
        partial_value = jnp.einsum(
            "kcpj,kcpg->jg", restricted, corner_marks, precision=lax.Precision.HIGHEST
        )
        neumann_part = apply_local(weighted, neumann, selector_half, selector_full)
        solved = coarse_solve(partial_value, coarse_inverse)
        picked = jnp.einsum("jg,kcpg->kcpj", solved, corner_marks, precision=lax.Precision.HIGHEST)
        correction = jnp.einsum("kcpj,kcpfn->kcfjn", picked, basis, precision=lax.Precision.HIGHEST)
        update = assemble(weights * (neumann_part + correction))
        solution = solution + damping * update
    return solution


def solution(mesh):
    in_specs = (
        P("sub", "wide", None, None, None),
        P(),
        P("sub", "wide", None),
        P("sub", "wide", None, None),
        P("sub", "wide", None, None),
        P("sub", "wide", None, None, None),
        P("sub", "wide", None),
        P("wide", None),
    )
    out_specs = P("sub", "wide", None, None, None)
    return jax.shard_map(body, mesh=mesh, in_specs=in_specs, out_specs=out_specs, check_vma=False)
```

profile of v0, /device:TPU:4, one launch (start us, length us, event | category | flops | bytes accessed | tf_op | source)
XLA Modules:
  0.0 250.2 jit_solution(4208679977386832550)
XLA Ops:
  0.9 3.5 %collective-permute-start = (f32[1,64,128]{2,1,0:T(8,128)S(1)}, f32[1,64,128]{2,1,0:T(8,128)S(1)}, u32[]{:S(2)}, u32[]{:S(2)}) collective-permute-start(f32[1,64,128]{2,1,0:T(8,128)S(1)} %get-tuple-element.47), channel_id=1, source_target_pairs={{0,8},{8,16},{16,24},{1,9},{9,17},{17,25},{2,10},{10,18},{18,26},{... | collective-permute-start | bytes 98312 | tf_op jit(solution)/shard_map/ppermute | solution.py:18
  6.4 4.5 %collective-permute-start.3 = (f32[1,1,64,128]{3,2,1,0:T(8,128)S(1)}, f32[1,1,64,128]{3,2,1,0:T(8,128)S(1)}, u32[]{:S(2)}, u32[]{:S(2)}) collective-permute-start(f32[1,1,64,128]{3,2,1,0:T(8,128)S(1)} %get-tuple-element.49), channel_id=1, source_target_pairs={{1,0},{2,1},{3,2},{4,3},{5,4},{6,5},{7,6},{9,8},{10,9},{11,10},{12... | collective-permute-start | bytes 98312 | tf_op jit(solution)/shard_map/ppermute | solution.py:20
  13.6 3.1 %collective-permute-done.1 = f32[1,64,128]{2,1,0:T(8,128)S(1)} collective-permute-done((f32[1,64,128]{2,1,0:T(8,128)S(1)}, f32[1,64,128]{2,1,0:T(8,128)S(1)}, u32[]{:S(2)}, u32[]{:S(2)}) %collective-permute-start.1) | collective-permute-done | bytes 32800 | tf_op jit(solution)/shard_map/ppermute | solution.py:20
  19.6 40.5 %psum.21 = f32[64,48]{0,1:T(8,128)S(1)} all-reduce(f32[64,48]{0,1:T(8,128)S(1)} %fusion.44), channel_id=1, replica_groups=mesh['sub'=4,'wide'=8] {'sub','wide'}, use_global_device_ids=true, to_apply=%region_0.1 | all-reduce | flops 3072 | bytes 24576 | tf_op jit(solution)/shard_map/psum | solution.py:56
  60.2 9.0 %all-gather = f32[8,6,64]{2,1,0:T(8,128)S(1)} all-gather(f32[1,6,64]{2,1,0:T(8,128)S(1)} %convolution_bitcast_fusion.6), channel_id=1, replica_groups=mesh['sub'=4,'wide'=8] {'wide'}, dimensions={0}, use_global_device_ids=true | all-gather | bytes 13824 | tf_op jit(solution)/shard_map/all_gather | solution.py:58
  70.4 2.3 collective-permute-start.6
  72.6 4.2 %collective-permute-start.7 = (f32[1,1,64,128]{3,2,1,0:T(8,128)S(1)}, f32[1,1,64,128]{3,2,1,0:T(8,128)S(1)}, u32[]{:S(2)}, u32[]{:S(2)}) collective-permute-start(f32[1,1,64,128]{3,2,1,0:T(8,128)S(1)} %get-tuple-element.41), channel_id=1, source_target_pairs={{1,0},{2,1},{3,2},{4,3},{5,4},{6,5},{7,6},{9,8},{10,9},{11,10},{12... | collective-permute-start | bytes 98312 | tf_op jit(solution)/shard_map/ppermute | solution.py:20
  80.8 4.2 %collective-permute-done.5 = f32[1,64,128]{2,1,0:T(8,128)S(1)} collective-permute-done((f32[1,64,128]{2,1,0:T(8,128)S(1)}, f32[1,64,128]{2,1,0:T(8,128)S(1)}, u32[]{:S(2)}, u32[]{:S(2)}) %collective-permute-start.5) | collective-permute-done | bytes 32800 | tf_op jit(solution)/shard_map/ppermute | solution.py:20
  87.9 4.5 %collective-permute-start.11 = (f32[1,1,64,128]{3,2,1,0:T(8,128)S(1)}, f32[1,1,64,128]{3,2,1,0:T(8,128)S(1)}, u32[]{:S(2)}, u32[]{:S(2)}) collective-permute-start(f32[1,1,64,128]{3,2,1,0:T(8,128)S(1)} %get-tuple-element.33), channel_id=1, source_target_pairs={{1,0},{2,1},{3,2},{4,3},{5,4},{6,5},{7,6},{9,8},{10,9},{11,10},{12... | collective-permute-start | bytes 98312 | tf_op jit(solution)/shard_map/ppermute | solution.py:20
  92.5 3.1 %collective-permute-start.8 = (f32[1,64,128]{2,1,0:T(8,128)S(1)}, f32[1,64,128]{2,1,0:T(8,128)S(1)}, u32[]{:S(2)}, u32[]{:S(2)}) collective-permute-start(f32[1,64,128]{2,1,0:T(8,128)S(1)} %get-tuple-element.31), channel_id=1, source_target_pairs={{0,8},{8,16},{16,24},{1,9},{9,17},{17,25},{2,10},{10,18},{18,26},{... | collective-permute-start | bytes 98312 | tf_op jit(solution)/shard_map/ppermute | solution.py:18
  97.1 4.2 %collective-permute-done.9 = f32[1,64,128]{2,1,0:T(8,128)S(1)} collective-permute-done((f32[1,64,128]{2,1,0:T(8,128)S(1)}, f32[1,64,128]{2,1,0:T(8,128)S(1)}, u32[]{:S(2)}, u32[]{:S(2)}) %collective-permute-start.9) | collective-permute-done | bytes 32800 | tf_op jit(solution)/shard_map/ppermute | solution.py:20
  102.3 40.3 %psum.22 = f32[64,48]{0,1:T(8,128)S(1)} all-reduce(f32[64,48]{0,1:T(8,128)S(1)} %fusion.43), channel_id=1, replica_groups=mesh['sub'=4,'wide'=8] {'sub','wide'}, use_global_device_ids=true, to_apply=%region_1.2 | all-reduce | flops 3072 | bytes 24576 | tf_op jit(solution)/shard_map/psum | solution.py:56
  142.7 9.5 %all-gather.1 = f32[8,6,64]{2,1,0:T(8,128)S(1)} all-gather(f32[1,6,64]{2,1,0:T(8,128)S(1)} %convolution_bitcast_fusion.5), channel_id=1, replica_groups=mesh['sub'=4,'wide'=8] {'wide'}, dimensions={0}, use_global_device_ids=true | all-gather | bytes 13824 | tf_op jit(solution)/shard_map/all_gather | solution.py:58
  153.3 2.3 collective-permute-start.14
  155.5 4.2 %collective-permute-start.15 = (f32[1,1,64,128]{3,2,1,0:T(8,128)S(1)}, f32[1,1,64,128]{3,2,1,0:T(8,128)S(1)}, u32[]{:S(2)}, u32[]{:S(2)}) collective-permute-start(f32[1,1,64,128]{3,2,1,0:T(8,128)S(1)} %get-tuple-element.25), channel_id=1, source_target_pairs={{1,0},{2,1},{3,2},{4,3},{5,4},{6,5},{7,6},{9,8},{10,9},{11,10},{12... | collective-permute-start | bytes 98312 | tf_op jit(solution)/shard_map/ppermute | solution.py:20
  163.3 4.2 %collective-permute-done.13 = f32[1,64,128]{2,1,0:T(8,128)S(1)} collective-permute-done((f32[1,64,128]{2,1,0:T(8,128)S(1)}, f32[1,64,128]{2,1,0:T(8,128)S(1)}, u32[]{:S(2)}, u32[]{:S(2)}) %collective-permute-start.13) | collective-permute-done | bytes 32800 | tf_op jit(solution)/shard_map/ppermute | solution.py:20
  170.4 4.5 %collective-permute-start.19 = (f32[1,1,64,128]{3,2,1,0:T(8,128)S(1)}, f32[1,1,64,128]{3,2,1,0:T(8,128)S(1)}, u32[]{:S(2)}, u32[]{:S(2)}) collective-permute-start(f32[1,1,64,128]{3,2,1,0:T(8,128)S(1)} %get-tuple-element.17), channel_id=1, source_target_pairs={{1,0},{2,1},{3,2},{4,3},{5,4},{6,5},{7,6},{9,8},{10,9},{11,10},{12... | collective-permute-start | bytes 98312 | tf_op jit(solution)/shard_map/ppermute | solution.py:20
  175.0 2.6 %collective-permute-start.16 = (f32[1,64,128]{2,1,0:T(8,128)S(1)}, f32[1,64,128]{2,1,0:T(8,128)S(1)}, u32[]{:S(2)}, u32[]{:S(2)}) collective-permute-start(f32[1,64,128]{2,1,0:T(8,128)S(1)} %get-tuple-element.15), channel_id=1, source_target_pairs={{0,8},{8,16},{16,24},{1,9},{9,17},{17,25},{2,10},{10,18},{18,26},{... | collective-permute-start | bytes 98312 | tf_op jit(solution)/shard_map/ppermute | solution.py:18
  179.1 4.2 %collective-permute-done.17 = f32[1,64,128]{2,1,0:T(8,128)S(1)} collective-permute-done((f32[1,64,128]{2,1,0:T(8,128)S(1)}, f32[1,64,128]{2,1,0:T(8,128)S(1)}, u32[]{:S(2)}, u32[]{:S(2)}) %collective-permute-start.17) | collective-permute-done | bytes 32800 | tf_op jit(solution)/shard_map/ppermute | solution.py:20
  184.9 40.3 %psum.23 = f32[64,48]{0,1:T(8,128)S(1)} all-reduce(f32[64,48]{0,1:T(8,128)S(1)} %fusion.42), channel_id=1, replica_groups=mesh['sub'=4,'wide'=8] {'sub','wide'}, use_global_device_ids=true, to_apply=%region_2.3 | all-reduce | flops 3072 | bytes 24576 | tf_op jit(solution)/shard_map/psum | solution.py:56
  225.2 9.5 %all-gather.2 = f32[8,6,64]{2,1,0:T(8,128)S(1)} all-gather(f32[1,6,64]{2,1,0:T(8,128)S(1)} %convolution_bitcast_fusion.4), channel_id=1, replica_groups=mesh['sub'=4,'wide'=8] {'wide'}, dimensions={0}, use_global_device_ids=true | all-gather | bytes 13824 | tf_op jit(solution)/shard_map/all_gather | solution.py:58
  235.3 2.3 collective-permute-start.22
  237.5 4.2 %collective-permute-start.23 = (f32[1,1,64,128]{3,2,1,0:T(8,128)S(1)}, f32[1,1,64,128]{3,2,1,0:T(8,128)S(1)}, u32[]{:S(2)}, u32[]{:S(2)}) collective-permute-start(f32[1,1,64,128]{3,2,1,0:T(8,128)S(1)} %get-tuple-element.9), channel_id=1, source_target_pairs={{1,0},{2,1},{3,2},{4,3},{5,4},{6,5},{7,6},{9,8},{10,9},{11,10},{12... | collective-permute-start | bytes 98312 | tf_op jit(solution)/shard_map/ppermute | solution.py:20
  245.2 4.2 %collective-permute-done.21 = f32[1,64,128]{2,1,0:T(8,128)S(1)} collective-permute-done((f32[1,64,128]{2,1,0:T(8,128)S(1)}, f32[1,64,128]{2,1,0:T(8,128)S(1)}, u32[]{:S(2)}, u32[]{:S(2)}) %collective-permute-start.21) | collective-permute-done | bytes 32800 | tf_op jit(solution)/shard_map/ppermute | solution.py:20
  (112 shorter events, 34.0 us)
Async XLA Ops:
  0.9 12.7 %collective-permute-start = (f32[1,64,128]{2,1,0:T(8,128)S(1)}, f32[1,64,128]{2,1,0:T(8,128)S(1)}, u32[]{:S(2)}, u32[]{:S(2)}) collective-permute-start(f32[1,64,128]{2,1,0:T(8,128)S(1)} %get-tuple-element.47), channel_id=1, source_target_pairs={{0,8},{8,16},{16,24},{1,9},{9,17},{17,25},{2,10},{10,18},{18,26},{... | collective-permute-start | bytes 98312 | tf_op jit(solution)/shard_map/ppermute | solution.py:18
  4.4 9.1 %collective-permute-start.2 = (f32[1,1,64,128]{3,2,1,0:T(8,128)S(1)}, f32[1,1,64,128]{3,2,1,0:T(8,128)S(1)}, u32[]{:S(2)}, u32[]{:S(2)}) collective-permute-start(f32[1,1,64,128]{3,2,1,0:T(8,128)S(1)} %get-tuple-element.48), channel_id=1, source_target_pairs={{0,1},{1,2},{2,3},{3,4},{4,5},{5,6},{6,7},{8,9},{9,10},{10,11},{11... | collective-permute-start | bytes 98312 | tf_op jit(solution)/shard_map/ppermute | solution.py:18
  6.4 7.2 %collective-permute-start.3 = (f32[1,1,64,128]{3,2,1,0:T(8,128)S(1)}, f32[1,1,64,128]{3,2,1,0:T(8,128)S(1)}, u32[]{:S(2)}, u32[]{:S(2)}) collective-permute-start(f32[1,1,64,128]{3,2,1,0:T(8,128)S(1)} %get-tuple-element.49), channel_id=1, source_target_pairs={{1,0},{2,1},{3,2},{4,3},{5,4},{6,5},{7,6},{9,8},{10,9},{11,10},{12... | collective-permute-start | bytes 98312 | tf_op jit(solution)/shard_map/ppermute | solution.py:20
  10.9 5.8 %collective-permute-start.1 = (f32[1,64,128]{2,1,0:T(8,128)S(1)}, f32[1,64,128]{2,1,0:T(8,128)S(1)}, u32[]{:S(2)}, u32[]{:S(2)}) collective-permute-start(f32[1,64,128]{2,1,0:T(8,128)S(1)} %get-tuple-element.50), channel_id=1, source_target_pairs={{8,0},{16,8},{24,16},{9,1},{17,9},{25,17},{10,2},{18,10},{26,18},{... | collective-permute-start | bytes 98312 | tf_op jit(solution)/shard_map/ppermute | solution.py:20
  70.4 10.2 %collective-permute-start.6 = (f32[1,1,64,128]{3,2,1,0:T(8,128)S(1)}, f32[1,1,64,128]{3,2,1,0:T(8,128)S(1)}, u32[]{:S(2)}, u32[]{:S(2)}) collective-permute-start(f32[1,1,64,128]{3,2,1,0:T(8,128)S(1)} %get-tuple-element.40), channel_id=1, source_target_pairs={{0,1},{1,2},{2,3},{3,4},{4,5},{5,6},{6,7},{8,9},{9,10},{10,11},{11... | collective-permute-start | bytes 98312 | tf_op jit(solution)/shard_map/ppermute | solution.py:18
  72.6 7.9 %collective-permute-start.7 = (f32[1,1,64,128]{3,2,1,0:T(8,128)S(1)}, f32[1,1,64,128]{3,2,1,0:T(8,128)S(1)}, u32[]{:S(2)}, u32[]{:S(2)}) collective-permute-start(f32[1,1,64,128]{3,2,1,0:T(8,128)S(1)} %get-tuple-element.41), channel_id=1, source_target_pairs={{1,0},{2,1},{3,2},{4,3},{5,4},{6,5},{7,6},{9,8},{10,9},{11,10},{12... | collective-permute-start | bytes 98312 | tf_op jit(solution)/shard_map/ppermute | solution.py:20
  77.1 3.7 %collective-permute-start.4 = (f32[1,64,128]{2,1,0:T(8,128)S(1)}, f32[1,64,128]{2,1,0:T(8,128)S(1)}, u32[]{:S(2)}, u32[]{:S(2)}) collective-permute-start(f32[1,64,128]{2,1,0:T(8,128)S(1)} %get-tuple-element.39), channel_id=1, source_target_pairs={{0,8},{8,16},{16,24},{1,9},{9,17},{17,25},{2,10},{10,18},{18,26},{... | collective-permute-start | bytes 98312 | tf_op jit(solution)/shard_map/ppermute | solution.py:18
  79.2 5.8 %collective-permute-start.5 = (f32[1,64,128]{2,1,0:T(8,128)S(1)}, f32[1,64,128]{2,1,0:T(8,128)S(1)}, u32[]{:S(2)}, u32[]{:S(2)}) collective-permute-start(f32[1,64,128]{2,1,0:T(8,128)S(1)} %get-tuple-element.42), channel_id=1, source_target_pairs={{8,0},{16,8},{24,16},{9,1},{17,9},{25,17},{10,2},{18,10},{26,18},{... | collective-permute-start | bytes 98312 | tf_op jit(solution)/shard_map/ppermute | solution.py:20
  86.0 10.8 %collective-permute-start.10 = (f32[1,1,64,128]{3,2,1,0:T(8,128)S(1)}, f32[1,1,64,128]{3,2,1,0:T(8,128)S(1)}, u32[]{:S(2)}, u32[]{:S(2)}) collective-permute-start(f32[1,1,64,128]{3,2,1,0:T(8,128)S(1)} %get-tuple-element.32), channel_id=1, source_target_pairs={{0,1},{1,2},{2,3},{3,4},{4,5},{5,6},{6,7},{8,9},{9,10},{10,11},{11... | collective-permute-start | bytes 98312 | tf_op jit(solution)/shard_map/ppermute | solution.py:18
  87.9 8.9 %collective-permute-start.11 = (f32[1,1,64,128]{3,2,1,0:T(8,128)S(1)}, f32[1,1,64,128]{3,2,1,0:T(8,128)S(1)}, u32[]{:S(2)}, u32[]{:S(2)}) collective-permute-start(f32[1,1,64,128]{3,2,1,0:T(8,128)S(1)} %get-tuple-element.33), channel_id=1, source_target_pairs={{1,0},{2,1},{3,2},{4,3},{5,4},{6,5},{7,6},{9,8},{10,9},{11,10},{12... | collective-permute-start | bytes 98312 | tf_op jit(solution)/shard_map/ppermute | solution.py:20
  92.5 4.6 %collective-permute-start.8 = (f32[1,64,128]{2,1,0:T(8,128)S(1)}, f32[1,64,128]{2,1,0:T(8,128)S(1)}, u32[]{:S(2)}, u32[]{:S(2)}) collective-permute-start(f32[1,64,128]{2,1,0:T(8,128)S(1)} %get-tuple-element.31), channel_id=1, source_target_pairs={{0,8},{8,16},{16,24},{1,9},{9,17},{17,25},{2,10},{10,18},{18,26},{... | collective-permute-start | bytes 98312 | tf_op jit(solution)/shard_map/ppermute | solution.py:18
  95.5 5.8 %collective-permute-start.9 = (f32[1,64,128]{2,1,0:T(8,128)S(1)}, f32[1,64,128]{2,1,0:T(8,128)S(1)}, u32[]{:S(2)}, u32[]{:S(2)}) collective-permute-start(f32[1,64,128]{2,1,0:T(8,128)S(1)} %get-tuple-element.34), channel_id=1, source_target_pairs={{8,0},{16,8},{24,16},{9,1},{17,9},{25,17},{10,2},{18,10},{26,18},{... | collective-permute-start | bytes 98312 | tf_op jit(solution)/shard_map/ppermute | solution.py:20
  153.3 9.7 %collective-permute-start.14 = (f32[1,1,64,128]{3,2,1,0:T(8,128)S(1)}, f32[1,1,64,128]{3,2,1,0:T(8,128)S(1)}, u32[]{:S(2)}, u32[]{:S(2)}) collective-permute-start(f32[1,1,64,128]{3,2,1,0:T(8,128)S(1)} %get-tuple-element.24), channel_id=1, source_target_pairs={{0,1},{1,2},{2,3},{3,4},{4,5},{5,6},{6,7},{8,9},{9,10},{10,11},{11... | collective-permute-start | bytes 98312 | tf_op jit(solution)/shard_map/ppermute | solution.py:18
  155.5 7.5 %collective-permute-start.15 = (f32[1,1,64,128]{3,2,1,0:T(8,128)S(1)}, f32[1,1,64,128]{3,2,1,0:T(8,128)S(1)}, u32[]{:S(2)}, u32[]{:S(2)}) collective-permute-start(f32[1,1,64,128]{3,2,1,0:T(8,128)S(1)} %get-tuple-element.25), channel_id=1, source_target_pairs={{1,0},{2,1},{3,2},{4,3},{5,4},{6,5},{7,6},{9,8},{10,9},{11,10},{12... | collective-permute-start | bytes 98312 | tf_op jit(solution)/shard_map/ppermute | solution.py:20
  159.8 3.5 %collective-permute-start.12 = (f32[1,64,128]{2,1,0:T(8,128)S(1)}, f32[1,64,128]{2,1,0:T(8,128)S(1)}, u32[]{:S(2)}, u32[]{:S(2)}) collective-permute-start(f32[1,64,128]{2,1,0:T(8,128)S(1)} %get-tuple-element.23), channel_id=1, source_target_pairs={{0,8},{8,16},{16,24},{1,9},{9,17},{17,25},{2,10},{10,18},{18,26},{... | collective-permute-start | bytes 98312 | tf_op jit(solution)/shard_map/ppermute | solution.py:18
  161.7 5.8 %collective-permute-start.13 = (f32[1,64,128]{2,1,0:T(8,128)S(1)}, f32[1,64,128]{2,1,0:T(8,128)S(1)}, u32[]{:S(2)}, u32[]{:S(2)}) collective-permute-start(f32[1,64,128]{2,1,0:T(8,128)S(1)} %get-tuple-element.26), channel_id=1, source_target_pairs={{8,0},{16,8},{24,16},{9,1},{17,9},{25,17},{10,2},{18,10},{26,18},{... | collective-permute-start | bytes 98312 | tf_op jit(solution)/shard_map/ppermute | solution.py:20
  168.5 10.3 %collective-permute-start.18 = (f32[1,1,64,128]{3,2,1,0:T(8,128)S(1)}, f32[1,1,64,128]{3,2,1,0:T(8,128)S(1)}, u32[]{:S(2)}, u32[]{:S(2)}) collective-permute-start(f32[1,1,64,128]{3,2,1,0:T(8,128)S(1)} %get-tuple-element.16), channel_id=1, source_target_pairs={{0,1},{1,2},{2,3},{3,4},{4,5},{5,6},{6,7},{8,9},{9,10},{10,11},{11... | collective-permute-start | bytes 98312 | tf_op jit(solution)/shard_map/ppermute | solution.py:18
  170.4 8.4 %collective-permute-start.19 = (f32[1,1,64,128]{3,2,1,0:T(8,128)S(1)}, f32[1,1,64,128]{3,2,1,0:T(8,128)S(1)}, u32[]{:S(2)}, u32[]{:S(2)}) collective-permute-start(f32[1,1,64,128]{3,2,1,0:T(8,128)S(1)} %get-tuple-element.17), channel_id=1, source_target_pairs={{1,0},{2,1},{3,2},{4,3},{5,4},{6,5},{7,6},{9,8},{10,9},{11,10},{12... | collective-permute-start | bytes 98312 | tf_op jit(solution)/shard_map/ppermute | solution.py:20
  175.0 4.1 %collective-permute-start.16 = (f32[1,64,128]{2,1,0:T(8,128)S(1)}, f32[1,64,128]{2,1,0:T(8,128)S(1)}, u32[]{:S(2)}, u32[]{:S(2)}) collective-permute-start(f32[1,64,128]{2,1,0:T(8,128)S(1)} %get-tuple-element.15), channel_id=1, source_target_pairs={{0,8},{8,16},{16,24},{1,9},{9,17},{17,25},{2,10},{10,18},{18,26},{... | collective-permute-start | bytes 98312 | tf_op jit(solution)/shard_map/ppermute | solution.py:18
  177.5 5.8 %collective-permute-start.17 = (f32[1,64,128]{2,1,0:T(8,128)S(1)}, f32[1,64,128]{2,1,0:T(8,128)S(1)}, u32[]{:S(2)}, u32[]{:S(2)}) collective-permute-start(f32[1,64,128]{2,1,0:T(8,128)S(1)} %get-tuple-element.18), channel_id=1, source_target_pairs={{8,0},{16,8},{24,16},{9,1},{17,9},{25,17},{10,2},{18,10},{26,18},{... | collective-permute-start | bytes 98312 | tf_op jit(solution)/shard_map/ppermute | solution.py:20
  235.3 9.7 %collective-permute-start.22 = (f32[1,1,64,128]{3,2,1,0:T(8,128)S(1)}, f32[1,1,64,128]{3,2,1,0:T(8,128)S(1)}, u32[]{:S(2)}, u32[]{:S(2)}) collective-permute-start(f32[1,1,64,128]{3,2,1,0:T(8,128)S(1)} %get-tuple-element.8), channel_id=1, source_target_pairs={{0,1},{1,2},{2,3},{3,4},{4,5},{5,6},{6,7},{8,9},{9,10},{10,11},{11... | collective-permute-start | bytes 98312 | tf_op jit(solution)/shard_map/ppermute | solution.py:18
  237.5 7.5 %collective-permute-start.23 = (f32[1,1,64,128]{3,2,1,0:T(8,128)S(1)}, f32[1,1,64,128]{3,2,1,0:T(8,128)S(1)}, u32[]{:S(2)}, u32[]{:S(2)}) collective-permute-start(f32[1,1,64,128]{3,2,1,0:T(8,128)S(1)} %get-tuple-element.9), channel_id=1, source_target_pairs={{1,0},{2,1},{3,2},{4,3},{5,4},{6,5},{7,6},{9,8},{10,9},{11,10},{12... | collective-permute-start | bytes 98312 | tf_op jit(solution)/shard_map/ppermute | solution.py:20
  241.7 3.5 %collective-permute-start.20 = (f32[1,64,128]{2,1,0:T(8,128)S(1)}, f32[1,64,128]{2,1,0:T(8,128)S(1)}, u32[]{:S(2)}, u32[]{:S(2)}) collective-permute-start(f32[1,64,128]{2,1,0:T(8,128)S(1)} %get-tuple-element.7), channel_id=1, source_target_pairs={{0,8},{8,16},{16,24},{1,9},{9,17},{17,25},{2,10},{10,18},{18,26},{... | collective-permute-start | bytes 98312 | tf_op jit(solution)/shard_map/ppermute | solution.py:18
  243.7 5.8 %collective-permute-start.21 = (f32[1,64,128]{2,1,0:T(8,128)S(1)}, f32[1,64,128]{2,1,0:T(8,128)S(1)}, u32[]{:S(2)}, u32[]{:S(2)}) collective-permute-start(f32[1,64,128]{2,1,0:T(8,128)S(1)} %get-tuple-element.10), channel_id=1, source_target_pairs={{8,0},{16,8},{24,16},{9,1},{17,9},{25,17},{10,2},{18,10},{26,18},{... | collective-permute-start | bytes 98312 | tf_op jit(solution)/shard_map/ppermute | solution.py:20
  (7 other events, 51.1 us)
where the time goes:
time: 251 us; the launch traced here: 250 us
  blocking collectives  149 us (59%)
  starting transfers between devices  61.6 us (25%)
  waiting for transfers between devices  25.5 us (10%)
  matrix products  7.57 us (3%)
  local copies, waits for them, and re-layouts  4.4 us (2%)
    psum x3, blocking collectives, coarse_solve(): assembled = lax.psum(partial_value, ('sub', 'wide'))  121 us
    ppermute x12, starting transfers between devices, with_halo(): lax.ppermute(head, axis, [((i + 1) % count, i) for i in range(ends)])  34 us
    all_gather x3, blocking collectives, coarse_solve(): return lax.all_gather(owned_rows, 'wide', axis=1, tiled=True)  28 us
    ppermute x12, starting transfers between devices, with_halo(): lax.ppermute(tail, axis, [(i, (i + 1) % count) for i in range(ends)])  27.6 us
    ppermute x12, waiting for transfers between devices, with_halo(): lax.ppermute(head, axis, [((i + 1) % count, i) for i in range(ends)])  24.3 us
  transfers between devices with their start and end apart: 24, of which 11 were waited for; matrix products, arithmetic and copies ran while one was open for 1% of the time, Pallas kernels for 0%

commit v1 on v0

--- a/solution.py
+++ b/solution.py
@@ -53,7 +53,7 @@
 
 
 def coarse_solve(partial_value, coarse_inverse):
-    assembled = lax.psum(partial_value, ("sub", "wide"))
+    assembled = lax.psum(lax.psum(partial_value, "sub"), "wide")
     owned_rows = jnp.dot(assembled, coarse_inverse.T, precision=lax.Precision.HIGHEST)
     return lax.all_gather(owned_rows, "wide", axis=1, tiled=True)
 

time: 251 us -> 242 us (0.964)
  blocking collectives: 149 us -> 139 us
    all_gather x3, blocking collectives: 28 us -> 21.2 us  [coarse_solve(): return lax.all_gather(owned_rows, 'wide', axis=1, tiled=True)]
    psum x3 -> x6, blocking collectives: 121 us -> 118 us  [coarse_solve(): assembled = lax.psum(lax.psum(partial_value, 'sub'), 'wide')]
where the time goes in v1:
time: 242 us; the launch traced here: 240 us
  blocking collectives  139 us (57%)
  starting transfers between devices  61.4 us (25%)
  waiting for transfers between devices  25.5 us (11%)
  matrix products  7.58 us (3%)
  local copies, waits for them, and re-layouts  4.4 us (2%)
    psum x6, blocking collectives, coarse_solve(): assembled = lax.psum(lax.psum(partial_value, 'sub'), 'wide')  118 us
    ppermute x12, starting transfers between devices, with_halo(): lax.ppermute(head, axis, [((i + 1) % count, i) for i in range(ends)])  34.2 us
    ppermute x12, starting transfers between devices, with_halo(): lax.ppermute(tail, axis, [(i, (i + 1) % count) for i in range(ends)])  27.1 us
    ppermute x12, waiting for transfers between devices, with_halo(): lax.ppermute(head, axis, [((i + 1) % count, i) for i in range(ends)])  24.3 us
    all_gather x3, blocking collectives, coarse_solve(): return lax.all_gather(owned_rows, 'wide', axis=1, tiled=True)  21.2 us
  transfers between devices with their start and end apart: 24, of which 11 were waited for; matrix products, arithmetic and copies ran while one was open for 1% of the time, Pallas kernels for 0%

profile of v1, /device:TPU:4, one launch (start us, length us, event | category | flops | bytes accessed | tf_op | source)
XLA Modules:
  0.0 239.9 jit_solution(5364389360063137836)
XLA Ops:
  0.9 3.5 %collective-permute-start = (f32[1,64,128]{2,1,0:T(8,128)S(1)}, f32[1,64,128]{2,1,0:T(8,128)S(1)}, u32[]{:S(2)}, u32[]{:S(2)}) collective-permute-start(f32[1,64,128]{2,1,0:T(8,128)S(1)} %get-tuple-element.47), channel_id=1, source_target_pairs={{0,8},{8,16},{16,24},{1,9},{9,17},{17,25},{2,10},{10,18},{18,26},{... | collective-permute-start | bytes 98312 | tf_op jit(solution)/shard_map/ppermute | solution.py:18
  6.4 4.5 %collective-permute-start.3 = (f32[1,1,64,128]{3,2,1,0:T(8,128)S(1)}, f32[1,1,64,128]{3,2,1,0:T(8,128)S(1)}, u32[]{:S(2)}, u32[]{:S(2)}) collective-permute-start(f32[1,1,64,128]{3,2,1,0:T(8,128)S(1)} %get-tuple-element.49), channel_id=1, source_target_pairs={{1,0},{2,1},{3,2},{4,3},{5,4},{6,5},{7,6},{9,8},{10,9},{11,10},{12... | collective-permute-start | bytes 98312 | tf_op jit(solution)/shard_map/ppermute | solution.py:20
  13.6 3.1 %collective-permute-done.1 = f32[1,64,128]{2,1,0:T(8,128)S(1)} collective-permute-done((f32[1,64,128]{2,1,0:T(8,128)S(1)}, f32[1,64,128]{2,1,0:T(8,128)S(1)}, u32[]{:S(2)}, u32[]{:S(2)}) %collective-permute-start.1) | collective-permute-done | bytes 32800 | tf_op jit(solution)/shard_map/ppermute | solution.py:20
  19.5 17.4 %psum.42 = f32[64,48]{0,1:T(8,128)S(1)} all-reduce(f32[64,48]{0,1:T(8,128)S(1)} %fusion.44), channel_id=1, replica_groups=mesh['sub'=4,'wide'=8] {'sub'}, use_global_device_ids=true, to_apply=%region_0.1 | all-reduce | flops 3072 | bytes 24576 | tf_op jit(solution)/shard_map/psum | solution.py:56
  37.0 22.4 %psum.43 = f32[64,48]{0,1:T(8,128)S(1)} all-reduce(f32[64,48]{0,1:T(8,128)S(1)} %psum.42), channel_id=1, replica_groups=mesh['sub'=4,'wide'=8] {'wide'}, use_global_device_ids=true, to_apply=%region_1.2 | all-reduce | flops 3072 | bytes 24576 | tf_op jit(solution)/shard_map/psum | solution.py:56
  59.5 7.0 %all-gather = f32[8,6,64]{2,1,0:T(8,128)S(1)} all-gather(f32[1,6,64]{2,1,0:T(8,128)S(1)} %convolution_bitcast_fusion.6), channel_id=1, replica_groups=mesh['sub'=4,'wide'=8] {'wide'}, dimensions={0}, use_global_device_ids=true | all-gather | bytes 13824 | tf_op jit(solution)/shard_map/all_gather | solution.py:58
  69.8 4.3 %collective-permute-start.7 = (f32[1,1,64,128]{3,2,1,0:T(8,128)S(1)}, f32[1,1,64,128]{3,2,1,0:T(8,128)S(1)}, u32[]{:S(2)}, u32[]{:S(2)}) collective-permute-start(f32[1,1,64,128]{3,2,1,0:T(8,128)S(1)} %get-tuple-element.41), channel_id=1, source_target_pairs={{1,0},{2,1},{3,2},{4,3},{5,4},{6,5},{7,6},{9,8},{10,9},{11,10},{12... | collective-permute-start | bytes 98312 | tf_op jit(solution)/shard_map/ppermute | solution.py:20
  77.2 4.2 %collective-permute-done.5 = f32[1,64,128]{2,1,0:T(8,128)S(1)} collective-permute-done((f32[1,64,128]{2,1,0:T(8,128)S(1)}, f32[1,64,128]{2,1,0:T(8,128)S(1)}, u32[]{:S(2)}, u32[]{:S(2)}) %collective-permute-start.5) | collective-permute-done | bytes 32800 | tf_op jit(solution)/shard_map/ppermute | solution.py:20
  84.3 4.5 %collective-permute-start.11 = (f32[1,1,64,128]{3,2,1,0:T(8,128)S(1)}, f32[1,1,64,128]{3,2,1,0:T(8,128)S(1)}, u32[]{:S(2)}, u32[]{:S(2)}) collective-permute-start(f32[1,1,64,128]{3,2,1,0:T(8,128)S(1)} %get-tuple-element.33), channel_id=1, source_target_pairs={{1,0},{2,1},{3,2},{4,3},{5,4},{6,5},{7,6},{9,8},{10,9},{11,10},{12... | collective-permute-start | bytes 98312 | tf_op jit(solution)/shard_map/ppermute | solution.py:20
  88.8 3.8 %collective-permute-start.8 = (f32[1,64,128]{2,1,0:T(8,128)S(1)}, f32[1,64,128]{2,1,0:T(8,128)S(1)}, u32[]{:S(2)}, u32[]{:S(2)}) collective-permute-start(f32[1,64,128]{2,1,0:T(8,128)S(1)} %get-tuple-element.31), channel_id=1, source_target_pairs={{0,8},{8,16},{16,24},{1,9},{9,17},{17,25},{2,10},{10,18},{18,26},{... | collective-permute-start | bytes 98312 | tf_op jit(solution)/shard_map/ppermute | solution.py:18
  94.2 4.2 %collective-permute-done.9 = f32[1,64,128]{2,1,0:T(8,128)S(1)} collective-permute-done((f32[1,64,128]{2,1,0:T(8,128)S(1)}, f32[1,64,128]{2,1,0:T(8,128)S(1)}, u32[]{:S(2)}, u32[]{:S(2)}) %collective-permute-start.9) | collective-permute-done | bytes 32800 | tf_op jit(solution)/shard_map/ppermute | solution.py:20
  99.4 16.0 %psum.44 = f32[64,48]{0,1:T(8,128)S(1)} all-reduce(f32[64,48]{0,1:T(8,128)S(1)} %fusion.43), channel_id=1, replica_groups=mesh['sub'=4,'wide'=8] {'sub'}, use_global_device_ids=true, to_apply=%region_2.3 | all-reduce | flops 3072 | bytes 24576 | tf_op jit(solution)/shard_map/psum | solution.py:56
  115.4 22.4 %psum.45 = f32[64,48]{0,1:T(8,128)S(1)} all-reduce(f32[64,48]{0,1:T(8,128)S(1)} %psum.44), channel_id=1, replica_groups=mesh['sub'=4,'wide'=8] {'wide'}, use_global_device_ids=true, to_apply=%region_3.4 | all-reduce | flops 3072 | bytes 24576 | tf_op jit(solution)/shard_map/psum | solution.py:56
  137.9 7.2 %all-gather.1 = f32[8,6,64]{2,1,0:T(8,128)S(1)} all-gather(f32[1,6,64]{2,1,0:T(8,128)S(1)} %convolution_bitcast_fusion.5), channel_id=1, replica_groups=mesh['sub'=4,'wide'=8] {'wide'}, dimensions={0}, use_global_device_ids=true | all-gather | bytes 13824 | tf_op jit(solution)/shard_map/all_gather | solution.py:58
  148.4 4.2 %collective-permute-start.15 = (f32[1,1,64,128]{3,2,1,0:T(8,128)S(1)}, f32[1,1,64,128]{3,2,1,0:T(8,128)S(1)}, u32[]{:S(2)}, u32[]{:S(2)}) collective-permute-start(f32[1,1,64,128]{3,2,1,0:T(8,128)S(1)} %get-tuple-element.25), channel_id=1, source_target_pairs={{1,0},{2,1},{3,2},{4,3},{5,4},{6,5},{7,6},{9,8},{10,9},{11,10},{12... | collective-permute-start | bytes 98312 | tf_op jit(solution)/shard_map/ppermute | solution.py:20
  156.1 4.2 %collective-permute-done.13 = f32[1,64,128]{2,1,0:T(8,128)S(1)} collective-permute-done((f32[1,64,128]{2,1,0:T(8,128)S(1)}, f32[1,64,128]{2,1,0:T(8,128)S(1)}, u32[]{:S(2)}, u32[]{:S(2)}) %collective-permute-start.13) | collective-permute-done | bytes 32800 | tf_op jit(solution)/shard_map/ppermute | solution.py:20
  163.2 4.5 %collective-permute-start.19 = (f32[1,1,64,128]{3,2,1,0:T(8,128)S(1)}, f32[1,1,64,128]{3,2,1,0:T(8,128)S(1)}, u32[]{:S(2)}, u32[]{:S(2)}) collective-permute-start(f32[1,1,64,128]{3,2,1,0:T(8,128)S(1)} %get-tuple-element.17), channel_id=1, source_target_pairs={{1,0},{2,1},{3,2},{4,3},{5,4},{6,5},{7,6},{9,8},{10,9},{11,10},{12... | collective-permute-start | bytes 98312 | tf_op jit(solution)/shard_map/ppermute | solution.py:20
  167.8 3.1 %collective-permute-start.16 = (f32[1,64,128]{2,1,0:T(8,128)S(1)}, f32[1,64,128]{2,1,0:T(8,128)S(1)}, u32[]{:S(2)}, u32[]{:S(2)}) collective-permute-start(f32[1,64,128]{2,1,0:T(8,128)S(1)} %get-tuple-element.15), channel_id=1, source_target_pairs={{0,8},{8,16},{16,24},{1,9},{9,17},{17,25},{2,10},{10,18},{18,26},{... | collective-permute-start | bytes 98312 | tf_op jit(solution)/shard_map/ppermute | solution.py:18
  172.5 4.2 %collective-permute-done.17 = f32[1,64,128]{2,1,0:T(8,128)S(1)} collective-permute-done((f32[1,64,128]{2,1,0:T(8,128)S(1)}, f32[1,64,128]{2,1,0:T(8,128)S(1)}, u32[]{:S(2)}, u32[]{:S(2)}) %collective-permute-start.17) | collective-permute-done | bytes 32800 | tf_op jit(solution)/shard_map/ppermute | solution.py:20
  178.2 17.4 %psum.46 = f32[64,48]{0,1:T(8,128)S(1)} all-reduce(f32[64,48]{0,1:T(8,128)S(1)} %fusion.42), channel_id=1, replica_groups=mesh['sub'=4,'wide'=8] {'sub'}, use_global_device_ids=true, to_apply=%region_4.5 | all-reduce | flops 3072 | bytes 24576 | tf_op jit(solution)/shard_map/psum | solution.py:56
  195.6 22.4 %psum.47 = f32[64,48]{0,1:T(8,128)S(1)} all-reduce(f32[64,48]{0,1:T(8,128)S(1)} %psum.46), channel_id=1, replica_groups=mesh['sub'=4,'wide'=8] {'wide'}, use_global_device_ids=true, to_apply=%region_5.6 | all-reduce | flops 3072 | bytes 24576 | tf_op jit(solution)/shard_map/psum | solution.py:56
  218.1 7.0 %all-gather.2 = f32[8,6,64]{2,1,0:T(8,128)S(1)} all-gather(f32[1,6,64]{2,1,0:T(8,128)S(1)} %convolution_bitcast_fusion.4), channel_id=1, replica_groups=mesh['sub'=4,'wide'=8] {'wide'}, dimensions={0}, use_global_device_ids=true | all-gather | bytes 13824 | tf_op jit(solution)/shard_map/all_gather | solution.py:58
  227.7 4.4 %collective-permute-start.23 = (f32[1,1,64,128]{3,2,1,0:T(8,128)S(1)}, f32[1,1,64,128]{3,2,1,0:T(8,128)S(1)}, u32[]{:S(2)}, u32[]{:S(2)}) collective-permute-start(f32[1,1,64,128]{3,2,1,0:T(8,128)S(1)} %get-tuple-element.9), channel_id=1, source_target_pairs={{1,0},{2,1},{3,2},{4,3},{5,4},{6,5},{7,6},{9,8},{10,9},{11,10},{12... | collective-permute-start | bytes 98312 | tf_op jit(solution)/shard_map/ppermute | solution.py:20
  235.0 4.2 %collective-permute-done.21 = f32[1,64,128]{2,1,0:T(8,128)S(1)} collective-permute-done((f32[1,64,128]{2,1,0:T(8,128)S(1)}, f32[1,64,128]{2,1,0:T(8,128)S(1)}, u32[]{:S(2)}, u32[]{:S(2)}) %collective-permute-start.21) | collective-permute-done | bytes 32800 | tf_op jit(solution)/shard_map/ppermute | solution.py:20
  (115 shorter events, 39.0 us)
Async XLA Ops:
  0.9 12.7 %collective-permute-start = (f32[1,64,128]{2,1,0:T(8,128)S(1)}, f32[1,64,128]{2,1,0:T(8,128)S(1)}, u32[]{:S(2)}, u32[]{:S(2)}) collective-permute-start(f32[1,64,128]{2,1,0:T(8,128)S(1)} %get-tuple-element.47), channel_id=1, source_target_pairs={{0,8},{8,16},{16,24},{1,9},{9,17},{17,25},{2,10},{10,18},{18,26},{... | collective-permute-start | bytes 98312 | tf_op jit(solution)/shard_map/ppermute | solution.py:18
  4.4 9.1 %collective-permute-start.2 = (f32[1,1,64,128]{3,2,1,0:T(8,128)S(1)}, f32[1,1,64,128]{3,2,1,0:T(8,128)S(1)}, u32[]{:S(2)}, u32[]{:S(2)}) collective-permute-start(f32[1,1,64,128]{3,2,1,0:T(8,128)S(1)} %get-tuple-element.48), channel_id=1, source_target_pairs={{0,1},{1,2},{2,3},{3,4},{4,5},{5,6},{6,7},{8,9},{9,10},{10,11},{11... | collective-permute-start | bytes 98312 | tf_op jit(solution)/shard_map/ppermute | solution.py:18
  6.4 7.2 %collective-permute-start.3 = (f32[1,1,64,128]{3,2,1,0:T(8,128)S(1)}, f32[1,1,64,128]{3,2,1,0:T(8,128)S(1)}, u32[]{:S(2)}, u32[]{:S(2)}) collective-permute-start(f32[1,1,64,128]{3,2,1,0:T(8,128)S(1)} %get-tuple-element.49), channel_id=1, source_target_pairs={{1,0},{2,1},{3,2},{4,3},{5,4},{6,5},{7,6},{9,8},{10,9},{11,10},{12... | collective-permute-start | bytes 98312 | tf_op jit(solution)/shard_map/ppermute | solution.py:20
  10.9 5.8 %collective-permute-start.1 = (f32[1,64,128]{2,1,0:T(8,128)S(1)}, f32[1,64,128]{2,1,0:T(8,128)S(1)}, u32[]{:S(2)}, u32[]{:S(2)}) collective-permute-start(f32[1,64,128]{2,1,0:T(8,128)S(1)} %get-tuple-element.50), channel_id=1, source_target_pairs={{8,0},{16,8},{24,16},{9,1},{17,9},{25,17},{10,2},{18,10},{26,18},{... | collective-permute-start | bytes 98312 | tf_op jit(solution)/shard_map/ppermute | solution.py:20
  67.6 9.3 %collective-permute-start.6 = (f32[1,1,64,128]{3,2,1,0:T(8,128)S(1)}, f32[1,1,64,128]{3,2,1,0:T(8,128)S(1)}, u32[]{:S(2)}, u32[]{:S(2)}) collective-permute-start(f32[1,1,64,128]{3,2,1,0:T(8,128)S(1)} %get-tuple-element.40), channel_id=1, source_target_pairs={{0,1},{1,2},{2,3},{3,4},{4,5},{5,6},{6,7},{8,9},{9,10},{10,11},{11... | collective-permute-start | bytes 98312 | tf_op jit(solution)/shard_map/ppermute | solution.py:18
  69.8 7.1 %collective-permute-start.7 = (f32[1,1,64,128]{3,2,1,0:T(8,128)S(1)}, f32[1,1,64,128]{3,2,1,0:T(8,128)S(1)}, u32[]{:S(2)}, u32[]{:S(2)}) collective-permute-start(f32[1,1,64,128]{3,2,1,0:T(8,128)S(1)} %get-tuple-element.41), channel_id=1, source_target_pairs={{1,0},{2,1},{3,2},{4,3},{5,4},{6,5},{7,6},{9,8},{10,9},{11,10},{12... | collective-permute-start | bytes 98312 | tf_op jit(solution)/shard_map/ppermute | solution.py:20
  74.3 2.9 %collective-permute-start.4 = (f32[1,64,128]{2,1,0:T(8,128)S(1)}, f32[1,64,128]{2,1,0:T(8,128)S(1)}, u32[]{:S(2)}, u32[]{:S(2)}) collective-permute-start(f32[1,64,128]{2,1,0:T(8,128)S(1)} %get-tuple-element.39), channel_id=1, source_target_pairs={{0,8},{8,16},{16,24},{1,9},{9,17},{17,25},{2,10},{10,18},{18,26},{... | collective-permute-start | bytes 98312 | tf_op jit(solution)/shard_map/ppermute | solution.py:18
  75.6 5.8 %collective-permute-start.5 = (f32[1,64,128]{2,1,0:T(8,128)S(1)}, f32[1,64,128]{2,1,0:T(8,128)S(1)}, u32[]{:S(2)}, u32[]{:S(2)}) collective-permute-start(f32[1,64,128]{2,1,0:T(8,128)S(1)} %get-tuple-element.42), channel_id=1, source_target_pairs={{8,0},{16,8},{24,16},{9,1},{17,9},{25,17},{10,2},{18,10},{26,18},{... | collective-permute-start | bytes 98312 | tf_op jit(solution)/shard_map/ppermute | solution.py:20
  82.4 11.6 %collective-permute-start.10 = (f32[1,1,64,128]{3,2,1,0:T(8,128)S(1)}, f32[1,1,64,128]{3,2,1,0:T(8,128)S(1)}, u32[]{:S(2)}, u32[]{:S(2)}) collective-permute-start(f32[1,1,64,128]{3,2,1,0:T(8,128)S(1)} %get-tuple-element.32), channel_id=1, source_target_pairs={{0,1},{1,2},{2,3},{3,4},{4,5},{5,6},{6,7},{8,9},{9,10},{10,11},{11... | collective-permute-start | bytes 98312 | tf_op jit(solution)/shard_map/ppermute | solution.py:18
  84.3 9.7 %collective-permute-start.11 = (f32[1,1,64,128]{3,2,1,0:T(8,128)S(1)}, f32[1,1,64,128]{3,2,1,0:T(8,128)S(1)}, u32[]{:S(2)}, u32[]{:S(2)}) collective-permute-start(f32[1,1,64,128]{3,2,1,0:T(8,128)S(1)} %get-tuple-element.33), channel_id=1, source_target_pairs={{1,0},{2,1},{3,2},{4,3},{5,4},{6,5},{7,6},{9,8},{10,9},{11,10},{12... | collective-permute-start | bytes 98312 | tf_op jit(solution)/shard_map/ppermute | solution.py:20
  88.8 5.4 %collective-permute-start.8 = (f32[1,64,128]{2,1,0:T(8,128)S(1)}, f32[1,64,128]{2,1,0:T(8,128)S(1)}, u32[]{:S(2)}, u32[]{:S(2)}) collective-permute-start(f32[1,64,128]{2,1,0:T(8,128)S(1)} %get-tuple-element.31), channel_id=1, source_target_pairs={{0,8},{8,16},{16,24},{1,9},{9,17},{17,25},{2,10},{10,18},{18,26},{... | collective-permute-start | bytes 98312 | tf_op jit(solution)/shard_map/ppermute | solution.py:18
  92.6 5.8 %collective-permute-start.9 = (f32[1,64,128]{2,1,0:T(8,128)S(1)}, f32[1,64,128]{2,1,0:T(8,128)S(1)}, u32[]{:S(2)}, u32[]{:S(2)}) collective-permute-start(f32[1,64,128]{2,1,0:T(8,128)S(1)} %get-tuple-element.34), channel_id=1, source_target_pairs={{8,0},{16,8},{24,16},{9,1},{17,9},{25,17},{10,2},{18,10},{26,18},{... | collective-permute-start | bytes 98312 | tf_op jit(solution)/shard_map/ppermute | solution.py:20
  146.2 9.6 %collective-permute-start.14 = (f32[1,1,64,128]{3,2,1,0:T(8,128)S(1)}, f32[1,1,64,128]{3,2,1,0:T(8,128)S(1)}, u32[]{:S(2)}, u32[]{:S(2)}) collective-permute-start(f32[1,1,64,128]{3,2,1,0:T(8,128)S(1)} %get-tuple-element.24), channel_id=1, source_target_pairs={{0,1},{1,2},{2,3},{3,4},{4,5},{5,6},{6,7},{8,9},{9,10},{10,11},{11... | collective-permute-start | bytes 98312 | tf_op jit(solution)/shard_map/ppermute | solution.py:18
  148.4 7.4 %collective-permute-start.15 = (f32[1,1,64,128]{3,2,1,0:T(8,128)S(1)}, f32[1,1,64,128]{3,2,1,0:T(8,128)S(1)}, u32[]{:S(2)}, u32[]{:S(2)}) collective-permute-start(f32[1,1,64,128]{3,2,1,0:T(8,128)S(1)} %get-tuple-element.25), channel_id=1, source_target_pairs={{1,0},{2,1},{3,2},{4,3},{5,4},{6,5},{7,6},{9,8},{10,9},{11,10},{12... | collective-permute-start | bytes 98312 | tf_op jit(solution)/shard_map/ppermute | solution.py:20
  152.7 3.4 %collective-permute-start.12 = (f32[1,64,128]{2,1,0:T(8,128)S(1)}, f32[1,64,128]{2,1,0:T(8,128)S(1)}, u32[]{:S(2)}, u32[]{:S(2)}) collective-permute-start(f32[1,64,128]{2,1,0:T(8,128)S(1)} %get-tuple-element.23), channel_id=1, source_target_pairs={{0,8},{8,16},{16,24},{1,9},{9,17},{17,25},{2,10},{10,18},{18,26},{... | collective-permute-start | bytes 98312 | tf_op jit(solution)/shard_map/ppermute | solution.py:18
  154.5 5.8 %collective-permute-start.13 = (f32[1,64,128]{2,1,0:T(8,128)S(1)}, f32[1,64,128]{2,1,0:T(8,128)S(1)}, u32[]{:S(2)}, u32[]{:S(2)}) collective-permute-start(f32[1,64,128]{2,1,0:T(8,128)S(1)} %get-tuple-element.26), channel_id=1, source_target_pairs={{8,0},{16,8},{24,16},{9,1},{17,9},{25,17},{10,2},{18,10},{26,18},{... | collective-permute-start | bytes 98312 | tf_op jit(solution)/shard_map/ppermute | solution.py:20
  161.3 10.9 %collective-permute-start.18 = (f32[1,1,64,128]{3,2,1,0:T(8,128)S(1)}, f32[1,1,64,128]{3,2,1,0:T(8,128)S(1)}, u32[]{:S(2)}, u32[]{:S(2)}) collective-permute-start(f32[1,1,64,128]{3,2,1,0:T(8,128)S(1)} %get-tuple-element.16), channel_id=1, source_target_pairs={{0,1},{1,2},{2,3},{3,4},{4,5},{5,6},{6,7},{8,9},{9,10},{10,11},{11... | collective-permute-start | bytes 98312 | tf_op jit(solution)/shard_map/ppermute | solution.py:18
  163.2 9.0 %collective-permute-start.19 = (f32[1,1,64,128]{3,2,1,0:T(8,128)S(1)}, f32[1,1,64,128]{3,2,1,0:T(8,128)S(1)}, u32[]{:S(2)}, u32[]{:S(2)}) collective-permute-start(f32[1,1,64,128]{3,2,1,0:T(8,128)S(1)} %get-tuple-element.17), channel_id=1, source_target_pairs={{1,0},{2,1},{3,2},{4,3},{5,4},{6,5},{7,6},{9,8},{10,9},{11,10},{12... | collective-permute-start | bytes 98312 | tf_op jit(solution)/shard_map/ppermute | solution.py:20
  167.8 4.7 %collective-permute-start.16 = (f32[1,64,128]{2,1,0:T(8,128)S(1)}, f32[1,64,128]{2,1,0:T(8,128)S(1)}, u32[]{:S(2)}, u32[]{:S(2)}) collective-permute-start(f32[1,64,128]{2,1,0:T(8,128)S(1)} %get-tuple-element.15), channel_id=1, source_target_pairs={{0,8},{8,16},{16,24},{1,9},{9,17},{17,25},{2,10},{10,18},{18,26},{... | collective-permute-start | bytes 98312 | tf_op jit(solution)/shard_map/ppermute | solution.py:18
  170.9 5.8 %collective-permute-start.17 = (f32[1,64,128]{2,1,0:T(8,128)S(1)}, f32[1,64,128]{2,1,0:T(8,128)S(1)}, u32[]{:S(2)}, u32[]{:S(2)}) collective-permute-start(f32[1,64,128]{2,1,0:T(8,128)S(1)} %get-tuple-element.18), channel_id=1, source_target_pairs={{8,0},{16,8},{24,16},{9,1},{17,9},{25,17},{10,2},{18,10},{26,18},{... | collective-permute-start | bytes 98312 | tf_op jit(solution)/shard_map/ppermute | solution.py:20
  225.6 9.1 %collective-permute-start.22 = (f32[1,1,64,128]{3,2,1,0:T(8,128)S(1)}, f32[1,1,64,128]{3,2,1,0:T(8,128)S(1)}, u32[]{:S(2)}, u32[]{:S(2)}) collective-permute-start(f32[1,1,64,128]{3,2,1,0:T(8,128)S(1)} %get-tuple-element.8), channel_id=1, source_target_pairs={{0,1},{1,2},{2,3},{3,4},{4,5},{5,6},{6,7},{8,9},{9,10},{10,11},{11... | collective-permute-start | bytes 98312 | tf_op jit(solution)/shard_map/ppermute | solution.py:18
  227.7 7.0 %collective-permute-start.23 = (f32[1,1,64,128]{3,2,1,0:T(8,128)S(1)}, f32[1,1,64,128]{3,2,1,0:T(8,128)S(1)}, u32[]{:S(2)}, u32[]{:S(2)}) collective-permute-start(f32[1,1,64,128]{3,2,1,0:T(8,128)S(1)} %get-tuple-element.9), channel_id=1, source_target_pairs={{1,0},{2,1},{3,2},{4,3},{5,4},{6,5},{7,6},{9,8},{10,9},{11,10},{12... | collective-permute-start | bytes 98312 | tf_op jit(solution)/shard_map/ppermute | solution.py:20
  232.1 2.9 %collective-permute-start.20 = (f32[1,64,128]{2,1,0:T(8,128)S(1)}, f32[1,64,128]{2,1,0:T(8,128)S(1)}, u32[]{:S(2)}, u32[]{:S(2)}) collective-permute-start(f32[1,64,128]{2,1,0:T(8,128)S(1)} %get-tuple-element.7), channel_id=1, source_target_pairs={{0,8},{8,16},{16,24},{1,9},{9,17},{17,25},{2,10},{10,18},{18,26},{... | collective-permute-start | bytes 98312 | tf_op jit(solution)/shard_map/ppermute | solution.py:18
  233.4 5.8 %collective-permute-start.21 = (f32[1,64,128]{2,1,0:T(8,128)S(1)}, f32[1,64,128]{2,1,0:T(8,128)S(1)}, u32[]{:S(2)}, u32[]{:S(2)}) collective-permute-start(f32[1,64,128]{2,1,0:T(8,128)S(1)} %get-tuple-element.10), channel_id=1, source_target_pairs={{8,0},{16,8},{24,16},{9,1},{17,9},{25,17},{10,2},{18,10},{26,18},{... | collective-permute-start | bytes 98312 | tf_op jit(solution)/shard_map/ppermute | solution.py:20
  (7 other events, 33.0 us)
